TPU v7x, 128 devices: a whole 4x4x4 slice. The times are simulated.
128 devices in a mesh: dom: 64 (over y, z, x), head: 2 (over core).
Axes of the slice: x: 4, y: 4, z: 4, core: 2. Of those that a mesh axis runs over, the one named last changes fastest.
Arguments:
- vertex_state: bfloat16 [131072, 128], P('dom'), may hold values from -6 to 6
- link_state_slotted: bfloat16 [786432, 128], P('dom'), may hold values from -6 to 6
- source_vertex_ids: int32 [786432], P('dom'), may hold values from 0 to 4095
- target_vertex_ids: int32 [786432], P('dom'), may hold values from 0 to 2047
- active_link_tally: int32 [64], P('dom'), may hold values from 6144 to 12288, as said below
- halo_outgoing_ids: int32 [64, 4, 512], P('dom'), may hold values from 0 to 2047
- link_layer_alpha: bfloat16 [384, 128], replicated, may hold values from -0.3125 to 0.3125
- link_layer_beta: bfloat16 [128, 128], replicated, may hold values from -0.5 to 0.5
- link_layer_gamma: bfloat16 [128, 128], replicated, may hold values from -0.5 to 0.5
- link_scale_factor: float32 [128], replicated, may hold values from 0.25 to 1.75
- vertex_layer_alpha: bfloat16 [256, 128], replicated, may hold values from -0.375 to 0.375
- vertex_layer_beta: bfloat16 [128, 128], replicated, may hold values from -0.5 to 0.5
- vertex_layer_gamma: bfloat16 [128, 128], replicated, may hold values from -0.5 to 0.5
- vertex_scale_factor: float32 [128], replicated, may hold values from 0.25 to 1.75
- focus_scale_factor: float32 [128], replicated, may hold values from 0.25 to 1.75
- vertex_content_factor: bfloat16 [128, 128], P(None, 'head'), may hold values from -0.5 to 0.5
- cluster_affinity_factor: bfloat16 [128, 512], P(None, 'head'), may hold values from -0.5 to 0.5
- softness_level: float32 [8], P('head'), may hold values from 0.15 to 2, as said below
- cluster_probe_lookup: float32 [2, 8, 16, 16], P(None, 'head'), may hold values from -8 to 8
- cluster_content_linear: float32 [8, 16, 16], P('head'), may hold values from -1.5 to 1.5
- closing_linear_factor: bfloat16 [128, 128], P('head'), may hold values from -0.5 to 0.5
Outputs:
- result: bfloat16 [131072, 128], P('dom')
Inputs may be any that keep to these rules, and one draw needn't show every extreme that they name: `active_link_tally`: each count lies between half the slots and all of them; in every draw some partition's slots are all valid. `softness_level`: positive.
All inputs are finite; a program needn't handle non-finite values.
Results may differ from a plain program's by a relative error of at most 0.0085.
Values may be sent and summed in bfloat16 or wider, within the bound.
A program may use at most 64 MiB of HBM per device.

v0:
```python
import math

import jax
import jax.numpy as jnp
from jax import lax
from jax.sharding import PartitionSpec as P

HEAD_DIM = 16
GROUPS_PER_LANE = 64


def passed_along(value, axis, steps):
    count = lax.axis_size(axis)
    first, last = (max(0, -steps), min(count, count - steps))
    return lax.ppermute(value, axis, [(source, source + steps) for source in range(first, last)])


def layer_norm(values, gain_row):
    row_mean = jnp.mean(values, axis=-1, keepdims=True)
    centred = values - row_mean
    row_var = jnp.mean(centred * centred, axis=-1, keepdims=True)
    return centred * lax.rsqrt(row_var + 1e-05) * gain_row


def node_section(
    own_rows,
    summed_b,
    vertex_layer_alpha,
    vertex_layer_beta,
    vertex_layer_gamma,
    vertex_scale_factor,
):
    feature_width = own_rows.shape[1]
    node_pre = jnp.dot(
        own_rows, vertex_layer_alpha[:feature_width], preferred_element_type=jnp.float32
    )
    node_pre = node_pre + jnp.dot(
        summed_b, vertex_layer_alpha[feature_width:], preferred_element_type=jnp.float32
    )
    node_one = jax.nn.silu(node_pre).astype(jnp.bfloat16)
    node_two = jax.nn.silu(
        jnp.dot(node_one, vertex_layer_beta, preferred_element_type=jnp.float32)
    ).astype(jnp.bfloat16)
    node_three = jnp.dot(node_two, vertex_layer_gamma, preferred_element_type=jnp.float32)
    return (own_rows.astype(jnp.float32) + layer_norm(node_three, vertex_scale_factor)).astype(
        jnp.bfloat16
    )


def slice_partial_terms(
    refreshed_vertices,
    focus_scale_factor,
    vertex_content_factor,
    cluster_affinity_factor,
    softness_level,
):
    count_of_rows = refreshed_vertices.shape[0]
    domain_channel_split = softness_level.shape[0]
    standardised_entries = layer_norm(
        refreshed_vertices.astype(jnp.float32), focus_scale_factor
    ).astype(jnp.bfloat16)
    values = jnp.dot(
        standardised_entries, vertex_content_factor, preferred_element_type=jnp.float32
    ).astype(jnp.bfloat16)
    cluster_affinities = jnp.dot(
        standardised_entries, cluster_affinity_factor, preferred_element_type=jnp.float32
    )
    cluster_affinities = (
        cluster_affinities.reshape(count_of_rows, domain_channel_split, GROUPS_PER_LANE)
        / softness_level[None, :, None]
    )
    weights = jax.nn.softmax(cluster_affinities, axis=-1)
    weights_b = weights.astype(jnp.bfloat16)
    numer = jnp.einsum(
        "nhs,nhc->hsc",
        weights_b,
        values.reshape(count_of_rows, domain_channel_split, HEAD_DIM),
        preferred_element_type=jnp.float32,
    )
    denom = jnp.sum(weights, axis=0)
    return (weights_b, numer, denom)


def slice_mixing(numer, denom, cluster_probe_lookup, cluster_content_linear):
    tokens = numer / denom[:, :, None]
    highest = lax.Precision.HIGHEST
    query = jnp.einsum("hsc,hcd->hsd", tokens, cluster_probe_lookup[0], precision=highest)
    keys = jnp.einsum("hsc,hcd->hsd", tokens, cluster_probe_lookup[1], precision=highest)
    carried = jnp.einsum("hsc,hcd->hsd", tokens, cluster_content_linear, precision=highest)
    scores = jnp.einsum("hsd,htd->hst", query, keys, precision=highest) / math.sqrt(HEAD_DIM)
    mixing = jax.nn.softmax(scores, axis=-1)
    return jnp.einsum("hst,htd->hsd", mixing, carried, precision=highest).astype(jnp.bfloat16)


def attend_rows(weights_b, slice_out):
    count_of_rows = weights_b.shape[0]
    domain_channel_split = weights_b.shape[1]
    attended = jnp.einsum("nhs,hsd->nhd", weights_b, slice_out, preferred_element_type=jnp.float32)
    return attended.reshape(count_of_rows, domain_channel_split * HEAD_DIM).astype(jnp.bfloat16)


def pick_rows(table, row_ids):
    table_ids = jnp.arange(table.shape[0], dtype=jnp.int32)
    selector = (row_ids[:, None] == table_ids[None, :]).astype(jnp.bfloat16)
    return jnp.dot(selector, table, preferred_element_type=jnp.float32).astype(jnp.bfloat16)


def body(
    vertex_state,
    link_state_slotted,
    source_vertex_ids,
    target_vertex_ids,
    active_link_tally,
    halo_outgoing_ids,
    link_layer_alpha,
    link_layer_beta,
    link_layer_gamma,
    link_scale_factor,
    vertex_layer_alpha,
    vertex_layer_beta,
    vertex_layer_gamma,
    vertex_scale_factor,
    focus_scale_factor,
    vertex_content_factor,
    cluster_affinity_factor,
    softness_level,
    cluster_probe_lookup,
    cluster_content_linear,
    closing_linear_factor,
):
    node_count = vertex_state.shape[0]
    feature_width = vertex_state.shape[1]
    capacity = link_state_slotted.shape[0]
    offsets = (1, -1, 2, -2)
    pieces = [vertex_state]
    for neighbour in range(4):
        outgoing = pick_rows(vertex_state, halo_outgoing_ids[0, neighbour])
        pieces.append(passed_along(outgoing, "dom", offsets[neighbour]))
    extended = jnp.concatenate(pieces, axis=0)
    extended_ids = jnp.arange(extended.shape[0], dtype=jnp.int32)
    node_ids = jnp.arange(node_count, dtype=jnp.int32)
    block_rows = min(node_count, 1024)
    share = capacity // lax.axis_size("head")
    first_row = lax.axis_index("head") * share
    edge_rows = lax.dynamic_slice_in_dim(link_state_slotted, first_row, share, 0)
    send_rows = lax.dynamic_slice_in_dim(source_vertex_ids, first_row, share, 0)
    recv_rows = lax.dynamic_slice_in_dim(target_vertex_ids, first_row, share, 0)
    turns = edge_rows.shape[0] // block_rows
    edge_blocks = edge_rows.reshape(turns, block_rows, feature_width)
    send_blocks = send_rows.reshape(turns, block_rows)
    recv_blocks = recv_rows.reshape(turns, block_rows)

    def step(total, item):
        edge_part, send_part, recv_part, turn = item
        send_hot = (send_part[:, None] == extended_ids[None, :]).astype(jnp.bfloat16)
        recv_hot = (recv_part[:, None] == node_ids[None, :]).astype(jnp.bfloat16)
        sender_rows = jnp.dot(send_hot, extended, preferred_element_type=jnp.float32).astype(
            jnp.bfloat16
        )
        receiver_rows = jnp.dot(recv_hot, vertex_state, preferred_element_type=jnp.float32).astype(
            jnp.bfloat16
        )
        pre = jnp.dot(
            edge_part, link_layer_alpha[:feature_width], preferred_element_type=jnp.float32
        )
        pre = pre + jnp.dot(
            sender_rows,
            link_layer_alpha[feature_width : 2 * feature_width],
            preferred_element_type=jnp.float32,
        )
        pre = pre + jnp.dot(
            receiver_rows, link_layer_alpha[2 * feature_width :], preferred_element_type=jnp.float32
        )
        first = jax.nn.silu(pre).astype(jnp.bfloat16)
        second = jax.nn.silu(
            jnp.dot(first, link_layer_beta, preferred_element_type=jnp.float32)
        ).astype(jnp.bfloat16)
        third = jnp.dot(second, link_layer_gamma, preferred_element_type=jnp.float32)
        edge_new = (edge_part.astype(jnp.float32) + layer_norm(third, link_scale_factor)).astype(
            jnp.bfloat16
        )
        position = first_row + turn * block_rows + jnp.arange(block_rows, dtype=jnp.int32)
        live = position < active_link_tally[0]
        messages = jnp.where(live[:, None], edge_new, jnp.zeros_like(edge_new))
        gathered = lax.dot_general(
            recv_hot, messages, (((0,), (0,)), ((), ())), preferred_element_type=jnp.float32
        )
        return (total + gathered, None)

    start = jnp.zeros((node_count, feature_width), jnp.float32)
    total, unused = lax.scan(
        step, start, (edge_blocks, send_blocks, recv_blocks, jnp.arange(turns, dtype=jnp.int32))
    )
    summed = lax.psum(total, "head")
    refreshed_vertices = node_section(
        vertex_state,
        summed.astype(jnp.bfloat16),
        vertex_layer_alpha,
        vertex_layer_beta,
        vertex_layer_gamma,
        vertex_scale_factor,
    )
    weights_b, numer, denom = slice_partial_terms(
        refreshed_vertices,
        focus_scale_factor,
        vertex_content_factor,
        cluster_affinity_factor,
        softness_level,
    )
    numer, denom = lax.psum((numer, denom), "dom")
    slice_out = slice_mixing(numer, denom, cluster_probe_lookup, cluster_content_linear)
    attended = attend_rows(weights_b, slice_out)
    projected = lax.psum(
        jnp.dot(attended, closing_linear_factor, preferred_element_type=jnp.float32).astype(
            jnp.bfloat16
        ),
        "head",
    ).astype(jnp.float32)
    return (refreshed_vertices.astype(jnp.float32) + projected).astype(jnp.bfloat16)


def solution(mesh):
    in_specs = (
        P("dom", None),
        P("dom", None),
        P("dom"),
        P("dom"),
        P("dom"),
        P("dom", None, None),
        P(),
        P(),
        P(),
        P(),
        P(),
        P(),
        P(),
        P(),
        P(),
        P(None, "head"),
        P(None, "head"),
        P("head"),
        P(None, "head", None, None),
        P("head", None, None),
        P("head", None),
    )
    out_specs = P("dom", None)
    return jax.shard_map(body, mesh=mesh, in_specs=in_specs, out_specs=out_specs, check_vma=False)
```

profile of v0, /device:TPU:1, one launch (start us, length us, event | category | flops | bytes accessed | tf_op | source)
XLA Modules:
  0.0 577.4 jit_solution(17982283348616390801)
XLA Ops:
  10.1 4.6 collective-permute-start
  19.0 4.9 collective-permute-start.2
  41.1 129.9 %while.11 = (s32[]{:T(128)}, f32[2048,128]{1,0:T(8,128)}, s32[6,1024]{1,0:T(8,128)}, s32[6]{0:T(128)S(1)}, s32[]{:T(128)}, /*index=5*/s32[1]{0:T(128)}, bf16[6,1...) while((s32[]{:T(128)}, f32[2048,128]{1,0:T(8,128)}, ...), condition=%wide.region_3.4_spmd.clone, body=%wide.region_0.3_spmd.clone.sunk | while | flops 2329545728 | bytes 9669339 | solution.py:191
  43.9 5.2 convolution_add_fusion.4
  49.0 3.6 multiply_convert_fusion.6
  58.8 3.7 fusion.136
  65.2 5.2 convolution_add_fusion.4
  70.4 3.6 multiply_convert_fusion.6
  80.1 4.0 fusion.136
  86.9 5.2 convolution_add_fusion.4
  92.1 3.6 multiply_convert_fusion.6
  101.8 4.0 fusion.136
  108.6 5.2 convolution_add_fusion.4
  113.8 3.6 multiply_convert_fusion.6
  123.5 4.0 fusion.136
  130.3 5.2 convolution_add_fusion.4
  135.5 3.6 multiply_convert_fusion.6
  145.3 4.0 fusion.136
  152.0 5.2 convolution_add_fusion.4
  157.2 3.6 multiply_convert_fusion.6
  167.0 4.0 fusion.136
  171.0 8.8 %all-reduce.5 = bf16[2048,128]{1,0:T(8,128)(2,1)} all-reduce(f32[2048,128]{1,0:T(8,128)} %get-tuple-element.87), channel_id=1, replica_groups=mesh['dom'=64,'head'=2] {'head'}, use_global_device_ids=true, to_apply=%region_4.5 | all-reduce | flops 262144 | bytes 1572864 | tf_op jit(solution)/shard_map/psum | solution.py:194
  191.6 296.4 %all-reduce = (f32[4,64,16]{1,2,0:T(8,128)S(1)}, f32[4,64]{1,0:T(4,128)S(1)}) all-reduce(f32[4,64,16]{1,2,0:T(8,128)S(1)} %fusion.78, f32[4,64]{1,0:T(4,128)S(1)} %reduce_sum.89), channel_id=1, replica_groups=mesh['dom'=64,'head'=2] {'dom'}, use_global_device_ids=true, to_apply=%region_11.12 | all-reduce | flops 4352 | bytes 34816 | tf_op jit(solution)/shard_map/psum | solution.py:210
  493.2 73.2 %all-reduce.4.cloned.1.call-done = bf16[2048,128]{0,1:T(8,128)(2,1)} async-done(((bf16[2048,128]{0,1:T(8,128)(2,1)}), bf16[2048,128]{0,1:T(8,128)(2,1)}) %all-reduce.4.cloned.1.call-update) | async-done | bytes 524304 | tf_op jit(solution)/shard_map/psum | solution.py:213
  (151 shorter events, 95.2 us)
Async XLA Ops:
  6.5 22.4 %copy-start = (bf16[12288,128]{1,0:T(8,128)(2,1)S(1)}, bf16[12288,128]{1,0:T(8,128)(2,1)}, u32[]{:S(2)}) copy-start(bf16[12288,128]{1,0:T(8,128)(2,1)} %param.24) | copy-start | bytes 9437188
  6.5 559.8 %all-reduce.4.cloned.1.call-start = ((), (), s32[]{:S(2)}) async-start(), calls=%async_computation | async-start | bytes 1048576 | tf_op jit(solution)/shard_map/psum | solution.py:213
  6.5 8.2 %copy-start.3 = (bf16[2048,128]{1,0:T(8,128)(2,1)S(1)}, bf16[2048,128]{1,0:T(8,128)(2,1)}, u32[]{:S(2)}) copy-start(bf16[2048,128]{1,0:T(8,128)(2,1)} %param.23) | copy-start | bytes 1572868
  10.1 26.5 %collective-permute-start = (bf16[512,128]{1,0:T(8,128)(2,1)}, bf16[512,128]{1,0:T(8,128)(2,1)}, u32[]{:S(2)}, u32[]{:S(2)}) collective-permute-start(bf16[512,128]{1,0:T(8,128)(2,1)} %fusion.49), channel_id=1, source_target_pairs={{0,2},{2,4},{4,6},{6,8},{8,10},{10,12},{12,14},{14,16},{16,18},{18... | collective-permute-start | bytes 393224 | tf_op jit(solution)/shard_map/ppermute | solution.py:15
  16.2 22.0 %collective-permute-start.1 = (bf16[512,128]{1,0:T(8,128)(2,1)}, bf16[512,128]{1,0:T(8,128)(2,1)}, u32[]{:S(2)}, u32[]{:S(2)}) collective-permute-start(bf16[512,128]{1,0:T(8,128)(2,1)} %fusion.48), channel_id=1, source_target_pairs={{2,0},{4,2},{6,4},{8,6},{10,8},{12,10},{14,12},{16,14},{18,16},{20... | collective-permute-start | bytes 393224 | tf_op jit(solution)/shard_map/ppermute | solution.py:15
  17.5 9.2 %copy-start.10 = (bf16[256,128]{1,0:T(8,128)(2,1)S(1)}, bf16[256,128]{1,0:T(8,128)(2,1)}, u32[]{:S(2)}) copy-start(bf16[256,128]{1,0:T(8,128)(2,1)} %param.33) | copy-start | bytes 196612
  19.0 20.7 %collective-permute-start.2 = (bf16[512,128]{1,0:T(8,128)(2,1)}, bf16[512,128]{1,0:T(8,128)(2,1)S(1)}, u32[]{:S(2)}, u32[]{:S(2)}) collective-permute-start(bf16[512,128]{1,0:T(8,128)(2,1)} %fusion.47), channel_id=1, source_target_pairs={{0,4},{2,6},{4,8},{6,10},{8,12},{10,14},{12,16},{14,18},{16,20},{1... | collective-permute-start | bytes 393224 | tf_op jit(solution)/shard_map/ppermute | solution.py:15
  25.4 15.0 %collective-permute-start.3 = (bf16[512,128]{1,0:T(8,128)(2,1)}, bf16[512,128]{1,0:T(8,128)(2,1)S(1)}, u32[]{:S(2)}, u32[]{:S(2)}) collective-permute-start(bf16[512,128]{1,0:T(8,128)(2,1)} %fusion.46), channel_id=1, source_target_pairs={{4,0},{6,2},{8,4},{10,6},{12,8},{14,10},{16,12},{18,14},{20,16},{2... | collective-permute-start | bytes 393224 | tf_op jit(solution)/shard_map/ppermute | solution.py:15
  29.0 1.3 copy-start.4
  29.0 6.9 %dynamic-slice-start = ((s32[12288]{0:T(1024)}, s32[]{:T(128)}), s32[6144]{0:T(1024)S(1)}, s32[]{:S(2)}) async-start(s32[12288]{0:T(1024)} %param.25, s32[]{:T(128)} %select_n.9), calls=%async_computation.1 | async-start | bytes 49664 | tf_op jit(solution)/shard_map/dynamic_slice | solution.py:146
  29.0 7.5 %copy-start.12 = (f32[4]{0:T(128)S(1)}, f32[4]{0:T(128)}, u32[]{:S(2)}) copy-start(f32[4]{0:T(128)} %param.40) | copy-start | bytes 52
  30.3 10.8 %copy-start.6 = (bf16[384,128]{1,0:T(8,128)(2,1)S(1)}, bf16[384,128]{1,0:T(8,128)(2,1)}, u32[]{:S(2)}) copy-start(bf16[384,128]{1,0:T(8,128)(2,1)} %param.29) | copy-start | bytes 294916
  30.3 10.8 %copy-start.17 = (f32[128]{0:T(128)S(1)}, f32[128]{0:T(128)}, u32[]{:S(2)}) copy-start(f32[128]{0:T(128)} %param.32) | copy-start | bytes 1540
  179.8 2.9 copy-start.8
  182.7 1.6 copy-start.5
  182.7 1.7 copy-start.13
  184.2 1.3 copy-start.7
  184.2 1.3 copy-start.14
  184.6 0.8 copy-start.2
  186.0 1.4 copy-start.1
  186.0 2.0 copy-start.16
  189.4 298.7 %copy-start.15 = (f32[2,4,16,16]{3,2,1,0:T(8,128)S(1)}, f32[2,4,16,16]{3,2,1,0:T(8,128)}, u32[]{:S(2)}) copy-start(f32[2,4,16,16]{3,2,1,0:T(8,128)} %param.41) | copy-start | bytes 24580
  189.4 299.1 %copy-start.9 = (f32[4,16,16]{2,1,0:T(8,128)S(1)}, f32[4,16,16]{2,1,0:T(8,128)}, u32[]{:S(2)}) copy-start(f32[4,16,16]{2,1,0:T(8,128)} %param.42) | copy-start | bytes 12292
  489.8 2.2 copy-start.11
Sparse Core Ops, SparseCore 0:
  493.3 73.0 all-reduce.3
where the time goes:
time: 580 us; the launch traced here: 577 us
  blocking collectives  305 us (53%)
  matrix products  119 us (21%)
  waiting for transfers between devices  73.2 us (13%)
  local copies, waits for them, and re-layouts  35.9 us (6%)
  other arithmetic  14.5 us (2%)
  between operations  13.6 us (2%)
  starting transfers between devices  12 us (2%)
    psum x1, blocking collectives, body(): numer, denom = lax.psum((numer, denom), 'dom')  296 us
    psum x1, waiting for transfers between devices, body(): lax.psum(jnp.dot(attended, closing_linear_factor, preferred_element_type=...  73.2 us
    dot_general x6, matrix products, step(): jnp.dot(sender_rows, link_layer_alpha[feature_width:2 * feature_width], p...  31.1 us
    dot_general x6, matrix products, step(): lax.dot_general(recv_hot, messages, (((0,), (0,)), ((), ())), preferred_e...  23.8 us
    dot_general x6, matrix products, step(): jnp.dot(receiver_rows, link_layer_alpha[2 * feature_width:], preferred_el...  21.8 us
    dynamic_slice x24, local copies, waits for them, and re-layouts, body(): lax.scan(step, start, (edge_blocks, send_blocks, recv_blocks, jnp.arange(...  19.3 us
    dot_general x6, matrix products, step(): jnp.dot(second, link_layer_gamma, preferred_element_type=jnp.float32)  13.2 us
    ppermute x4, starting transfers between devices, passed_along(): lax.ppermute(value, axis, [(source, source + steps) for source in range(f...  12 us
  transfers between devices with their start and end apart: 5, of which 1 were waited for; matrix products, arithmetic and copies ran while one was open for 3% of the time, Pallas kernels for 0%

commit v1 on v0

--- a/solution.py
+++ b/solution.py
@@ -1,8 +1,11 @@
+import functools
 import math
 
 import jax
 import jax.numpy as jnp
 from jax import lax
+from jax.experimental import pallas as pl
+from jax.experimental.pallas import tpu as pltpu
 from jax.sharding import PartitionSpec as P
 
 HEAD_DIM = 16
@@ -13,6 +16,63 @@
     count = lax.axis_size(axis)
     first, last = (max(0, -steps), min(count, count - steps))
     return lax.ppermute(value, axis, [(source, source + steps) for source in range(first, last)])
+
+
+def _doubling_kernel(steps, x_ref, o_ref, inbox, send_sem, recv_sem):
+    me = lax.axis_index("dom")
+    partners = []
+    for k in range(steps):
+        span = 2**k
+        bit = (me // span) % 2
+        partners.append(me + span - 2 * span * bit)
+    barrier = pltpu.get_barrier_semaphore()
+    for partner in partners:
+        pl.semaphore_signal(
+            barrier, 1, device_id={"dom": partner}, device_id_type=pl.DeviceIdType.MESH
+        )
+    pl.semaphore_wait(barrier, steps)
+    for k in range(steps):
+        source = x_ref if k == 0 else o_ref
+        copy = pltpu.make_async_remote_copy(
+            src_ref=source,
+            dst_ref=inbox.at[k],
+            send_sem=send_sem.at[k],
+            recv_sem=recv_sem.at[k],
+            device_id={"dom": partners[k]},
+            device_id_type=pl.DeviceIdType.MESH,
+        )
+        copy.start()
+        copy.wait()
+        o_ref[...] = source[...] + inbox[k]
+
+
+def dom_sum(flat):
+    count = lax.axis_size("dom")
+    steps = count.bit_length() - 1
+    return pl.pallas_call(
+        functools.partial(_doubling_kernel, steps),
+        out_shape=jax.ShapeDtypeStruct(flat.shape, flat.dtype),
+        in_specs=[pl.BlockSpec(memory_space=pltpu.VMEM)],
+        out_specs=pl.BlockSpec(memory_space=pltpu.VMEM),
+        scratch_shapes=[
+            pltpu.VMEM((steps,) + flat.shape, flat.dtype),
+            pltpu.SemaphoreType.DMA((steps,)),
+            pltpu.SemaphoreType.DMA((steps,)),
+        ],
+        compiler_params=pltpu.CompilerParams(collective_id=0, has_side_effects=True),
+    )(flat)
+
+
+def psum_slices(numer, denom):
+    joined = jnp.concatenate([numer.reshape(-1), denom.reshape(-1)])
+    rows = -(-joined.shape[0] // 1024) * 8
+    padded = jnp.zeros((rows * 128,), joined.dtype).at[: joined.shape[0]].set(joined)
+    total = dom_sum(padded.reshape(rows, 128)).reshape(-1)
+    numer_size = numer.size
+    return (
+        total[:numer_size].reshape(numer.shape),
+        total[numer_size : numer_size + denom.size].reshape(denom.shape),
+    )
 
 
 def layer_norm(values, gain_row):
@@ -207,7 +267,7 @@
         cluster_affinity_factor,
         softness_level,
     )
-    numer, denom = lax.psum((numer, denom), "dom")
+    numer, denom = psum_slices(numer, denom)
     slice_out = slice_mixing(numer, denom, cluster_probe_lookup, cluster_content_linear)
     attended = attend_rows(weights_b, slice_out)
     projected = lax.psum(

time: 580 us -> 264 us (0.46)
  blocking collectives: 305 us -> 8.8 us
  waiting for transfers between devices: 73.2 us -> 29.7 us
  Pallas kernels: 0 us -> 24.5 us
    psum x1 -> x0, blocking collectives: 296 us -> none  [body(): numer, denom = lax.psum((numer, denom), 'dom')]
    psum x1, waiting for transfers between devices: 73.2 us -> 29.6 us  [body(): lax.psum(jnp.dot(attended, closing_linear_factor, preferred_element_type=...]
    pallas_call x0 -> x1, Pallas kernels: none -> 24.5 us  [dom_sum(): pl.pallas_call(functools.partial(_doubling_kernel, steps), out_shape=jax....]
  transfers between devices with their start and end apart: 5 -> 5, of which waited for: 1 -> 1; matrix products, arithmetic and copies ran while one was open for 3% -> 7% of each run, Pallas kernels for 0% -> 0%
where the time goes in v1:
time: 264 us; the launch traced here: 261 us
  matrix products  115 us (44%)
  local copies, waits for them, and re-layouts  37.1 us (14%)
  waiting for transfers between devices  29.7 us (11%)
  Pallas kernels  24.5 us (9%)
  other arithmetic  16.7 us (6%)
  between operations  13.7 us (5%)
  starting transfers between devices  12 us (5%)
  blocking collectives  8.8 us (3%)
  loops' own time  3.98 us (2%)
    dot_general x6, matrix products, step(): jnp.dot(sender_rows, link_layer_alpha[feature_width:2 * feature_width], p...  31.1 us
    psum x1, waiting for transfers between devices, body(): lax.psum(jnp.dot(attended, closing_linear_factor, preferred_element_type=...  29.6 us
    pallas_call x1, Pallas kernels, dom_sum(): pl.pallas_call(functools.partial(_doubling_kernel, steps), out_shape=jax....  24.5 us
    dot_general x6, matrix products, step(): lax.dot_general(recv_hot, messages, (((0,), (0,)), ((), ())), preferred_e...  23.8 us
    dot_general x6, matrix products, step(): jnp.dot(receiver_rows, link_layer_alpha[2 * feature_width:], preferred_el...  21.8 us
    dynamic_slice x24, local copies, waits for them, and re-layouts, body(): lax.scan(step, start, (edge_blocks, send_blocks, recv_blocks, jnp.arange(...  19.3 us
    dot_general x6, matrix products, step(): jnp.dot(second, link_layer_gamma, preferred_element_type=jnp.float32)  13.2 us
    ppermute x4, starting transfers between devices, passed_along(): lax.ppermute(value, axis, [(source, source + steps) for source in range(f...  12 us
  transfers between devices with their start and end apart: 5, of which 1 were waited for; matrix products, arithmetic and copies ran while one was open for 7% of the time, Pallas kernels for 0%

profile of v1, /device:TPU:1, one launch (start us, length us, event | category | flops | bytes accessed | tf_op | source)
XLA Modules:
  0.0 261.3 jit_solution(12139312678654210538)
XLA Ops:
  10.1 4.6 %collective-permute-start = (bf16[512,128]{1,0:T(8,128)(2,1)}, bf16[512,128]{1,0:T(8,128)(2,1)}, u32[]{:S(2)}, u32[]{:S(2)}) collective-permute-start(bf16[512,128]{1,0:T(8,128)(2,1)} %fusion.49), channel_id=1, source_target_pairs={{0,2},{2,4},{4,6},{6,8},{8,10},{10,12},{12,14},{14,16},{16,18},{18... | collective-permute-start | bytes 393224 | tf_op jit(solution)/shard_map/ppermute | solution.py:18
  19.0 4.9 %collective-permute-start.2 = (bf16[512,128]{1,0:T(8,128)(2,1)}, bf16[512,128]{1,0:T(8,128)(2,1)S(1)}, u32[]{:S(2)}, u32[]{:S(2)}) collective-permute-start(bf16[512,128]{1,0:T(8,128)(2,1)} %fusion.47), channel_id=1, source_target_pairs={{0,4},{2,6},{4,8},{6,10},{8,12},{10,14},{12,16},{14,18},{16,20},{1... | collective-permute-start | bytes 393224 | tf_op jit(solution)/shard_map/ppermute | solution.py:18
  41.1 129.9 %while.12 = (s32[]{:T(128)}, f32[2048,128]{1,0:T(8,128)}, s32[6,1024]{1,0:T(8,128)}, s32[6]{0:T(128)S(1)}, s32[]{:T(128)}, /*index=5*/s32[1]{0:T(128)}, bf16[6,1...) while((s32[]{:T(128)}, f32[2048,128]{1,0:T(8,128)}, ...), condition=%wide.region_3.4_spmd.clone, body=%wide.region_0.3_spmd.clone.sunk | while | flops 2329545728 | bytes 9669339 | solution.py:251
  43.9 5.2 %convolution_add_fusion.4 = f32[1024,128]{1,0:T(8,128)} fusion(f32[1024,128]{1,0:T(8,128)} %fusion.135, bf16[4096,128]{1,0:T(8,128)(2,1)} %get-tuple-element.343, s32[1024]{0:T(1024)S(1)} %bitcast.97, bf16[384,128]{1,0:T(8,128)(2,1)S(1)} %get-tuple-element.341), kind=kOutput, calls=%fused_computation.13.clone.1 | convolution fusion | flops 1111752704 | bytes 2134016 | tf_op jit(solution)/shard_map/while/body/eval_jaxpr/dot_general | solution.py:226
  49.0 3.6 %multiply_convert_fusion.6 = bf16[1024,128]{1,0:T(8,128)(2,1)} fusion(f32[1024,128]{1,0:T(8,128)} %convolution_add_fusion.4, bf16[2048,128]{1,0:T(8,128)(2,1)} %get-tuple-element.344, s32[1024]{0:T(1024)S(1)} %bitcast.95, bf16[384,128]{1,0:T(8,128)(2,1)S(1)} %get-tuple-element.341), kind=kOutput, calls=%fused_computation.19.clone.1 | convolution fusion | flops 573440000 | bytes 1347584 | tf_op jit(solution)/shard_map/while/body/eval_jaxpr/dot_general | solution.py:231
  58.8 3.7 %fusion.137 = f32[2048,128]{1,0:T(8,128)} fusion(s32[1024]{0:T(1024)S(1)} %bitcast.96, f32[2048,128]{1,0:T(8,128)} %get-tuple-element.318, pred[]{:T(512)S(6)} %compare.14, f32[1024,128]{0,1:T(8,128)} %get-tuple-element.298, bf16[1,1024,128]{1,2,0:T(8,128)(2,1)} %copy.34, f32[128]{0:T(128)S(1)} %get-tuple-element.347, ...), kind=kOutput, calls=%fused_computation.11.clone.1 | convolution fusion | flops 542507008 | bytes 2897409 | tf_op jit(solution)/shard_map/while/body/eval_jaxpr/dot_general | solution.py:245
  65.2 5.2 %convolution_add_fusion.4 = f32[1024,128]{1,0:T(8,128)} fusion(f32[1024,128]{1,0:T(8,128)} %fusion.135, bf16[4096,128]{1,0:T(8,128)(2,1)} %get-tuple-element.343, s32[1024]{0:T(1024)S(1)} %bitcast.97, bf16[384,128]{1,0:T(8,128)(2,1)S(1)} %get-tuple-element.341), kind=kOutput, calls=%fused_computation.13.clone.1 | convolution fusion | flops 1111752704 | bytes 2134016 | tf_op jit(solution)/shard_map/while/body/eval_jaxpr/dot_general | solution.py:226
  70.4 3.6 %multiply_convert_fusion.6 = bf16[1024,128]{1,0:T(8,128)(2,1)} fusion(f32[1024,128]{1,0:T(8,128)} %convolution_add_fusion.4, bf16[2048,128]{1,0:T(8,128)(2,1)} %get-tuple-element.344, s32[1024]{0:T(1024)S(1)} %bitcast.95, bf16[384,128]{1,0:T(8,128)(2,1)S(1)} %get-tuple-element.341), kind=kOutput, calls=%fused_computation.19.clone.1 | convolution fusion | flops 573440000 | bytes 1347584 | tf_op jit(solution)/shard_map/while/body/eval_jaxpr/dot_general | solution.py:231
  80.1 4.0 %fusion.137 = f32[2048,128]{1,0:T(8,128)} fusion(s32[1024]{0:T(1024)S(1)} %bitcast.96, f32[2048,128]{1,0:T(8,128)} %get-tuple-element.318, pred[]{:T(512)S(6)} %compare.14, f32[1024,128]{0,1:T(8,128)} %get-tuple-element.298, bf16[1,1024,128]{1,2,0:T(8,128)(2,1)} %copy.34, f32[128]{0:T(128)S(1)} %get-tuple-element.347, ...), kind=kOutput, calls=%fused_computation.11.clone.1 | convolution fusion | flops 542507008 | bytes 2897409 | tf_op jit(solution)/shard_map/while/body/eval_jaxpr/dot_general | solution.py:245
  86.9 5.2 %convolution_add_fusion.4 = f32[1024,128]{1,0:T(8,128)} fusion(f32[1024,128]{1,0:T(8,128)} %fusion.135, bf16[4096,128]{1,0:T(8,128)(2,1)} %get-tuple-element.343, s32[1024]{0:T(1024)S(1)} %bitcast.97, bf16[384,128]{1,0:T(8,128)(2,1)S(1)} %get-tuple-element.341), kind=kOutput, calls=%fused_computation.13.clone.1 | convolution fusion | flops 1111752704 | bytes 2134016 | tf_op jit(solution)/shard_map/while/body/eval_jaxpr/dot_general | solution.py:226
  92.1 3.6 %multiply_convert_fusion.6 = bf16[1024,128]{1,0:T(8,128)(2,1)} fusion(f32[1024,128]{1,0:T(8,128)} %convolution_add_fusion.4, bf16[2048,128]{1,0:T(8,128)(2,1)} %get-tuple-element.344, s32[1024]{0:T(1024)S(1)} %bitcast.95, bf16[384,128]{1,0:T(8,128)(2,1)S(1)} %get-tuple-element.341), kind=kOutput, calls=%fused_computation.19.clone.1 | convolution fusion | flops 573440000 | bytes 1347584 | tf_op jit(solution)/shard_map/while/body/eval_jaxpr/dot_general | solution.py:231
  101.8 4.0 %fusion.137 = f32[2048,128]{1,0:T(8,128)} fusion(s32[1024]{0:T(1024)S(1)} %bitcast.96, f32[2048,128]{1,0:T(8,128)} %get-tuple-element.318, pred[]{:T(512)S(6)} %compare.14, f32[1024,128]{0,1:T(8,128)} %get-tuple-element.298, bf16[1,1024,128]{1,2,0:T(8,128)(2,1)} %copy.34, f32[128]{0:T(128)S(1)} %get-tuple-element.347, ...), kind=kOutput, calls=%fused_computation.11.clone.1 | convolution fusion | flops 542507008 | bytes 2897409 | tf_op jit(solution)/shard_map/while/body/eval_jaxpr/dot_general | solution.py:245
  108.6 5.2 %convolution_add_fusion.4 = f32[1024,128]{1,0:T(8,128)} fusion(f32[1024,128]{1,0:T(8,128)} %fusion.135, bf16[4096,128]{1,0:T(8,128)(2,1)} %get-tuple-element.343, s32[1024]{0:T(1024)S(1)} %bitcast.97, bf16[384,128]{1,0:T(8,128)(2,1)S(1)} %get-tuple-element.341), kind=kOutput, calls=%fused_computation.13.clone.1 | convolution fusion | flops 1111752704 | bytes 2134016 | tf_op jit(solution)/shard_map/while/body/eval_jaxpr/dot_general | solution.py:226
  113.8 3.6 %multiply_convert_fusion.6 = bf16[1024,128]{1,0:T(8,128)(2,1)} fusion(f32[1024,128]{1,0:T(8,128)} %convolution_add_fusion.4, bf16[2048,128]{1,0:T(8,128)(2,1)} %get-tuple-element.344, s32[1024]{0:T(1024)S(1)} %bitcast.95, bf16[384,128]{1,0:T(8,128)(2,1)S(1)} %get-tuple-element.341), kind=kOutput, calls=%fused_computation.19.clone.1 | convolution fusion | flops 573440000 | bytes 1347584 | tf_op jit(solution)/shard_map/while/body/eval_jaxpr/dot_general | solution.py:231
  123.5 4.0 %fusion.137 = f32[2048,128]{1,0:T(8,128)} fusion(s32[1024]{0:T(1024)S(1)} %bitcast.96, f32[2048,128]{1,0:T(8,128)} %get-tuple-element.318, pred[]{:T(512)S(6)} %compare.14, f32[1024,128]{0,1:T(8,128)} %get-tuple-element.298, bf16[1,1024,128]{1,2,0:T(8,128)(2,1)} %copy.34, f32[128]{0:T(128)S(1)} %get-tuple-element.347, ...), kind=kOutput, calls=%fused_computation.11.clone.1 | convolution fusion | flops 542507008 | bytes 2897409 | tf_op jit(solution)/shard_map/while/body/eval_jaxpr/dot_general | solution.py:245
  130.3 5.2 %convolution_add_fusion.4 = f32[1024,128]{1,0:T(8,128)} fusion(f32[1024,128]{1,0:T(8,128)} %fusion.135, bf16[4096,128]{1,0:T(8,128)(2,1)} %get-tuple-element.343, s32[1024]{0:T(1024)S(1)} %bitcast.97, bf16[384,128]{1,0:T(8,128)(2,1)S(1)} %get-tuple-element.341), kind=kOutput, calls=%fused_computation.13.clone.1 | convolution fusion | flops 1111752704 | bytes 2134016 | tf_op jit(solution)/shard_map/while/body/eval_jaxpr/dot_general | solution.py:226
  135.5 3.6 %multiply_convert_fusion.6 = bf16[1024,128]{1,0:T(8,128)(2,1)} fusion(f32[1024,128]{1,0:T(8,128)} %convolution_add_fusion.4, bf16[2048,128]{1,0:T(8,128)(2,1)} %get-tuple-element.344, s32[1024]{0:T(1024)S(1)} %bitcast.95, bf16[384,128]{1,0:T(8,128)(2,1)S(1)} %get-tuple-element.341), kind=kOutput, calls=%fused_computation.19.clone.1 | convolution fusion | flops 573440000 | bytes 1347584 | tf_op jit(solution)/shard_map/while/body/eval_jaxpr/dot_general | solution.py:231
  145.3 4.0 %fusion.137 = f32[2048,128]{1,0:T(8,128)} fusion(s32[1024]{0:T(1024)S(1)} %bitcast.96, f32[2048,128]{1,0:T(8,128)} %get-tuple-element.318, pred[]{:T(512)S(6)} %compare.14, f32[1024,128]{0,1:T(8,128)} %get-tuple-element.298, bf16[1,1024,128]{1,2,0:T(8,128)(2,1)} %copy.34, f32[128]{0:T(128)S(1)} %get-tuple-element.347, ...), kind=kOutput, calls=%fused_computation.11.clone.1 | convolution fusion | flops 542507008 | bytes 2897409 | tf_op jit(solution)/shard_map/while/body/eval_jaxpr/dot_general | solution.py:245
  152.0 5.2 %convolution_add_fusion.4 = f32[1024,128]{1,0:T(8,128)} fusion(f32[1024,128]{1,0:T(8,128)} %fusion.135, bf16[4096,128]{1,0:T(8,128)(2,1)} %get-tuple-element.343, s32[1024]{0:T(1024)S(1)} %bitcast.97, bf16[384,128]{1,0:T(8,128)(2,1)S(1)} %get-tuple-element.341), kind=kOutput, calls=%fused_computation.13.clone.1 | convolution fusion | flops 1111752704 | bytes 2134016 | tf_op jit(solution)/shard_map/while/body/eval_jaxpr/dot_general | solution.py:226
  157.2 3.6 %multiply_convert_fusion.6 = bf16[1024,128]{1,0:T(8,128)(2,1)} fusion(f32[1024,128]{1,0:T(8,128)} %convolution_add_fusion.4, bf16[2048,128]{1,0:T(8,128)(2,1)} %get-tuple-element.344, s32[1024]{0:T(1024)S(1)} %bitcast.95, bf16[384,128]{1,0:T(8,128)(2,1)S(1)} %get-tuple-element.341), kind=kOutput, calls=%fused_computation.19.clone.1 | convolution fusion | flops 573440000 | bytes 1347584 | tf_op jit(solution)/shard_map/while/body/eval_jaxpr/dot_general | solution.py:231
  167.0 4.0 %fusion.137 = f32[2048,128]{1,0:T(8,128)} fusion(s32[1024]{0:T(1024)S(1)} %bitcast.96, f32[2048,128]{1,0:T(8,128)} %get-tuple-element.318, pred[]{:T(512)S(6)} %compare.14, f32[1024,128]{0,1:T(8,128)} %get-tuple-element.298, bf16[1,1024,128]{1,2,0:T(8,128)(2,1)} %copy.34, f32[128]{0:T(128)S(1)} %get-tuple-element.347, ...), kind=kOutput, calls=%fused_computation.11.clone.1 | convolution fusion | flops 542507008 | bytes 2897409 | tf_op jit(solution)/shard_map/while/body/eval_jaxpr/dot_general | solution.py:245
  171.0 8.8 %all-reduce.5 = bf16[2048,128]{1,0:T(8,128)(2,1)} all-reduce(f32[2048,128]{1,0:T(8,128)} %get-tuple-element.99), channel_id=1, replica_groups=mesh['dom'=64,'head'=2] {'head'}, use_global_device_ids=true, to_apply=%region_4.5 | all-reduce | flops 262144 | bytes 1572864 | tf_op jit(solution)/shard_map/psum | solution.py:254
  190.7 24.5 %shard_map.199 = f32[40,128]{1,0:T(8,128)} custom-call(f32[40,128]{1,0:T(8,128)} %fusion.75.x_ref), custom_call_target="tpu_custom_call" | custom-call | tf_op jit(solution)/shard_map/pallas_call | solution.py:52
  220.6 29.6 %all-reduce.4.cloned.1.call-done = bf16[2048,128]{0,1:T(8,128)(2,1)} async-done(((bf16[2048,128]{0,1:T(8,128)(2,1)}), bf16[2048,128]{0,1:T(8,128)(2,1)}) %all-reduce.4.cloned.1.call-update) | async-done | bytes 524304 | tf_op jit(solution)/shard_map/psum | solution.py:273
  (158 shorter events, 94.6 us)
Async XLA Ops:
  6.5 22.4 %copy-start = (bf16[12288,128]{1,0:T(8,128)(2,1)S(1)}, bf16[12288,128]{1,0:T(8,128)(2,1)}, u32[]{:S(2)}) copy-start(bf16[12288,128]{1,0:T(8,128)(2,1)} %param.26) | copy-start | bytes 9437188
  6.5 243.7 %all-reduce.4.cloned.1.call-start = ((), (), s32[]{:S(2)}) async-start(), calls=%async_computation | async-start | bytes 1048576 | tf_op jit(solution)/shard_map/psum | solution.py:273
  6.5 8.2 %copy-start.4 = (bf16[2048,128]{1,0:T(8,128)(2,1)S(1)}, bf16[2048,128]{1,0:T(8,128)(2,1)}, u32[]{:S(2)}) copy-start(bf16[2048,128]{1,0:T(8,128)(2,1)} %param.25) | copy-start | bytes 1572868
  10.1 26.5 %collective-permute-start = (bf16[512,128]{1,0:T(8,128)(2,1)}, bf16[512,128]{1,0:T(8,128)(2,1)}, u32[]{:S(2)}, u32[]{:S(2)}) collective-permute-start(bf16[512,128]{1,0:T(8,128)(2,1)} %fusion.49), channel_id=1, source_target_pairs={{0,2},{2,4},{4,6},{6,8},{8,10},{10,12},{12,14},{14,16},{16,18},{18... | collective-permute-start | bytes 393224 | tf_op jit(solution)/shard_map/ppermute | solution.py:18
  16.2 22.0 %collective-permute-start.1 = (bf16[512,128]{1,0:T(8,128)(2,1)}, bf16[512,128]{1,0:T(8,128)(2,1)}, u32[]{:S(2)}, u32[]{:S(2)}) collective-permute-start(bf16[512,128]{1,0:T(8,128)(2,1)} %fusion.48), channel_id=1, source_target_pairs={{2,0},{4,2},{6,4},{8,6},{10,8},{12,10},{14,12},{16,14},{18,16},{20... | collective-permute-start | bytes 393224 | tf_op jit(solution)/shard_map/ppermute | solution.py:18
  17.5 9.2 %copy-start.10 = (bf16[256,128]{1,0:T(8,128)(2,1)S(1)}, bf16[256,128]{1,0:T(8,128)(2,1)}, u32[]{:S(2)}) copy-start(bf16[256,128]{1,0:T(8,128)(2,1)} %param.35) | copy-start | bytes 196612
  19.0 20.7 %collective-permute-start.2 = (bf16[512,128]{1,0:T(8,128)(2,1)}, bf16[512,128]{1,0:T(8,128)(2,1)S(1)}, u32[]{:S(2)}, u32[]{:S(2)}) collective-permute-start(bf16[512,128]{1,0:T(8,128)(2,1)} %fusion.47), channel_id=1, source_target_pairs={{0,4},{2,6},{4,8},{6,10},{8,12},{10,14},{12,16},{14,18},{16,20},{1... | collective-permute-start | bytes 393224 | tf_op jit(solution)/shard_map/ppermute | solution.py:18
  25.4 15.0 %collective-permute-start.3 = (bf16[512,128]{1,0:T(8,128)(2,1)}, bf16[512,128]{1,0:T(8,128)(2,1)S(1)}, u32[]{:S(2)}, u32[]{:S(2)}) collective-permute-start(bf16[512,128]{1,0:T(8,128)(2,1)} %fusion.46), channel_id=1, source_target_pairs={{4,0},{6,2},{8,4},{10,6},{12,8},{14,10},{16,12},{18,14},{20,16},{2... | collective-permute-start | bytes 393224 | tf_op jit(solution)/shard_map/ppermute | solution.py:18
  29.0 1.3 copy-start.5
  29.0 6.9 %dynamic-slice-start = ((s32[12288]{0:T(1024)}, s32[]{:T(128)}), s32[6144]{0:T(1024)S(1)}, s32[]{:S(2)}) async-start(s32[12288]{0:T(1024)} %param.27, s32[]{:T(128)} %select_n.9), calls=%async_computation.1 | async-start | bytes 49664 | tf_op jit(solution)/shard_map/dynamic_slice | solution.py:206
  29.0 7.5 %copy-start.12 = (f32[4]{0:T(128)S(1)}, f32[4]{0:T(128)}, u32[]{:S(2)}) copy-start(f32[4]{0:T(128)} %param.42) | copy-start | bytes 52
  30.3 10.8 %copy-start.7 = (bf16[384,128]{1,0:T(8,128)(2,1)S(1)}, bf16[384,128]{1,0:T(8,128)(2,1)}, u32[]{:S(2)}) copy-start(bf16[384,128]{1,0:T(8,128)(2,1)} %param.31) | copy-start | bytes 294916
  30.3 10.8 %copy-start.18 = (f32[128]{0:T(128)S(1)}, f32[128]{0:T(128)}, u32[]{:S(2)}) copy-start(f32[128]{0:T(128)} %param.34) | copy-start | bytes 1540
  179.8 2.9 %copy-start.9 = (bf16[128,128]{1,0:T(8,128)(2,1)S(1)}, bf16[128,128]{1,0:T(8,128)(2,1)}, u32[]{:S(2)}) copy-start(bf16[128,128]{1,0:T(8,128)(2,1)} %param.37) | copy-start | bytes 98308
  182.7 1.7 copy-start.6
  182.7 1.7 copy-start.13
  184.2 0.7 copy-start.17
  184.3 0.9 copy-start.8
  184.7 1.1 copy-start.3
  185.8 1.4 copy-start.1
  187.7 29.0 %copy-start.15 = (f32[2,4,16,16]{3,2,1,0:T(8,128)S(1)}, f32[2,4,16,16]{3,2,1,0:T(8,128)}, u32[]{:S(2)}) copy-start(f32[2,4,16,16]{3,2,1,0:T(8,128)} %param.43) | copy-start | bytes 24580
  187.8 29.8 %copy-start.16 = (f32[4,16,16]{2,1,0:T(8,128)S(1)}, f32[4,16,16]{2,1,0:T(8,128)}, u32[]{:S(2)}) copy-start(f32[4,16,16]{2,1,0:T(8,128)} %param.44) | copy-start | bytes 12292
  216.7 2.0 copy-start.2
  218.7 0.7 copy-start.11
  (1 other events, 0.7 us)
Sparse Core Ops, SparseCore 0:
  220.8 29.4 all-reduce.3

commit v2 on v1

--- a/solution.py
+++ b/solution.py
@@ -270,12 +270,7 @@
     numer, denom = psum_slices(numer, denom)
     slice_out = slice_mixing(numer, denom, cluster_probe_lookup, cluster_content_linear)
     attended = attend_rows(weights_b, slice_out)
-    projected = lax.psum(
-        jnp.dot(attended, closing_linear_factor, preferred_element_type=jnp.float32).astype(
-            jnp.bfloat16
-        ),
-        "head",
-    ).astype(jnp.float32)
+    projected = jnp.dot(attended, closing_linear_factor, preferred_element_type=jnp.float32)
     return (refreshed_vertices.astype(jnp.float32) + projected).astype(jnp.bfloat16)
 
 
@@ -296,12 +291,12 @@
         P(),
         P(),
         P(),
-        P(None, "head"),
-        P(None, "head"),
-        P("head"),
-        P(None, "head", None, None),
-        P("head", None, None),
-        P("head", None),
+        P(),
+        P(),
+        P(),
+        P(),
+        P(),
+        P(),
     )
     out_specs = P("dom", None)
     return jax.shard_map(body, mesh=mesh, in_specs=in_specs, out_specs=out_specs, check_vma=False)

time: 264 us -> 257 us (0.973)
  the two profiles are of different devices: /device:TPU:1 before, /device:TPU:6 now
where the time goes in v2:
time: 257 us; the launch traced here: 254 us
  matrix products  122 us (47%)
  local copies, waits for them, and re-layouts  45.7 us (18%)
  Pallas kernels  30.3 us (12%)
  blocking collectives  21.4 us (8%)
  other arithmetic  17 us (7%)
  starting transfers between devices  13.3 us (5%)
  loops' own time  3.96 us (2%)
    dot_general x6, matrix products, step(): jnp.dot(sender_rows, link_layer_alpha[feature_width:2 * feature_width], p...  31.1 us
    pallas_call x1, Pallas kernels, dom_sum(): pl.pallas_call(functools.partial(_doubling_kernel, steps), out_shape=jax....  30.3 us
    dot_general x6, matrix products, step(): lax.dot_general(recv_hot, messages, (((0,), (0,)), ((), ())), preferred_e...  23.9 us
    dynamic_slice x24, local copies, waits for them, and re-layouts, body(): lax.scan(step, start, (edge_blocks, send_blocks, recv_blocks, jnp.arange(...  23.3 us
    dot_general x6, matrix products, step(): jnp.dot(receiver_rows, link_layer_alpha[2 * feature_width:], preferred_el...  21.7 us
    unnamed x5, blocking collectives  13.9 us
    ppermute x4, starting transfers between devices, passed_along(): lax.ppermute(value, axis, [(source, source + steps) for source in range(f...  13.3 us
    dot_general x6, matrix products, step(): jnp.dot(second, link_layer_gamma, preferred_element_type=jnp.float32)  13.2 us
  transfers between devices with their start and end apart: 4, of which 0 were waited for; matrix products, arithmetic and copies ran while one was open for 8% of the time, Pallas kernels for 0%

profile of v2, /device:TPU:6, one launch (start us, length us, event | category | flops | bytes accessed | tf_op | source)
XLA Modules:
  0.0 254.4 jit_solution(12771921459904730917)
XLA Ops:
  3.6 3.7 %collective-permute-start = (bf16[512,128]{1,0:T(8,128)(2,1)}, bf16[512,128]{1,0:T(8,128)(2,1)}, u32[]{:S(2)}, u32[]{:S(2)}) collective-permute-start(bf16[512,128]{1,0:T(8,128)(2,1)} %fusion.50), channel_id=1, source_target_pairs={{0,2},{2,4},{4,6},{6,8},{8,10},{10,12},{12,14},{14,16},{16,18},{18... | collective-permute-start | bytes 393224 | tf_op jit(solution)/shard_map/ppermute | solution.py:18
  13.5 4.7 %collective-permute-start.2 = (bf16[512,128]{1,0:T(8,128)(2,1)}, bf16[512,128]{1,0:T(8,128)(2,1)S(1)}, u32[]{:S(2)}, u32[]{:S(2)}) collective-permute-start(bf16[512,128]{1,0:T(8,128)(2,1)} %fusion.48), channel_id=1, source_target_pairs={{0,4},{2,6},{4,8},{6,10},{8,12},{10,14},{12,16},{14,18},{16,20},{1... | collective-permute-start | bytes 393224 | tf_op jit(solution)/shard_map/ppermute | solution.py:18
  40.4 3.3 %all-gather = bf16[128,128]{0,1:T(8,128)(2,1)} all-gather(bf16[128,64]{0,1:T(8,128)(2,1)} %param.40), channel_id=3, replica_groups=mesh['dom'=64,'head'=2] {'head'}, dimensions={1}, use_global_device_ids=true | all-gather | bytes 49152 | tf_op args[15]
  53.0 134.0 %while.12 = (s32[]{:T(128)}, f32[2048,128]{1,0:T(8,128)}, s32[6,1024]{1,0:T(8,128)S(1)}, s32[6]{0:T(128)}, s32[]{:T(128)}, /*index=5*/s32[1]{0:T(128)}, bf16[6,1...) while((s32[]{:T(128)}, f32[2048,128]{1,0:T(8,128)}, ...), condition=%wide.region_3.4_spmd.clone, body=%wide.region_0.3_spmd.clone.sunk | while | flops 2329545728 | bytes 9669339 | solution.py:251
  55.7 5.2 %convolution_add_fusion.5 = f32[1024,128]{1,0:T(8,128)} fusion(f32[1024,128]{1,0:T(8,128)} %fusion.131, bf16[4096,128]{1,0:T(8,128)(2,1)} %get-tuple-element.373, s32[1024]{0:T(1024)S(1)} %bitcast.98, bf16[384,128]{1,0:T(8,128)(2,1)S(1)} %get-tuple-element.371), kind=kOutput, calls=%fused_computation.13.clone.1 | convolution fusion | flops 1111752704 | bytes 2134016 | tf_op jit(solution)/shard_map/while/body/eval_jaxpr/dot_general | solution.py:226
  60.9 3.6 %multiply_convert_fusion.6 = bf16[1024,128]{1,0:T(8,128)(2,1)} fusion(f32[1024,128]{1,0:T(8,128)} %convolution_add_fusion.5, bf16[2048,128]{1,0:T(8,128)(2,1)} %get-tuple-element.374, s32[1024]{0:T(1024)S(1)} %bitcast.96, bf16[384,128]{1,0:T(8,128)(2,1)S(1)} %get-tuple-element.371), kind=kOutput, calls=%fused_computation.19.clone.1 | convolution fusion | flops 573440000 | bytes 1347584 | tf_op jit(solution)/shard_map/while/body/eval_jaxpr/dot_general | solution.py:231
  71.3 3.7 %fusion.133 = f32[2048,128]{1,0:T(8,128)} fusion(s32[1024]{0:T(1024)S(1)} %bitcast.97, f32[2048,128]{1,0:T(8,128)} %get-tuple-element.348, pred[]{:T(512)S(6)} %compare.14, f32[1024,128]{0,1:T(8,128)} %get-tuple-element.328, bf16[1,1024,128]{1,2,0:T(8,128)(2,1)} %copy.56, f32[128]{0:T(128)} %get-tuple-element.377, f32[1024]{0:T(1024)S(1)} %add_rsqrt_fusion.4, ...), kind=kOutput, calls=%fused_computation.11.clone.1 | convolution fusion | flops 542507008 | bytes 2897409 | tf_op jit(solution)/shard_map/while/body/eval_jaxpr/dot_general | solution.py:245
  77.7 5.2 %convolution_add_fusion.5 = f32[1024,128]{1,0:T(8,128)} fusion(f32[1024,128]{1,0:T(8,128)} %fusion.131, bf16[4096,128]{1,0:T(8,128)(2,1)} %get-tuple-element.373, s32[1024]{0:T(1024)S(1)} %bitcast.98, bf16[384,128]{1,0:T(8,128)(2,1)S(1)} %get-tuple-element.371), kind=kOutput, calls=%fused_computation.13.clone.1 | convolution fusion | flops 1111752704 | bytes 2134016 | tf_op jit(solution)/shard_map/while/body/eval_jaxpr/dot_general | solution.py:226
  82.9 3.6 %multiply_convert_fusion.6 = bf16[1024,128]{1,0:T(8,128)(2,1)} fusion(f32[1024,128]{1,0:T(8,128)} %convolution_add_fusion.5, bf16[2048,128]{1,0:T(8,128)(2,1)} %get-tuple-element.374, s32[1024]{0:T(1024)S(1)} %bitcast.96, bf16[384,128]{1,0:T(8,128)(2,1)S(1)} %get-tuple-element.371), kind=kOutput, calls=%fused_computation.19.clone.1 | convolution fusion | flops 573440000 | bytes 1347584 | tf_op jit(solution)/shard_map/while/body/eval_jaxpr/dot_general | solution.py:231
  93.3 4.0 %fusion.133 = f32[2048,128]{1,0:T(8,128)} fusion(s32[1024]{0:T(1024)S(1)} %bitcast.97, f32[2048,128]{1,0:T(8,128)} %get-tuple-element.348, pred[]{:T(512)S(6)} %compare.14, f32[1024,128]{0,1:T(8,128)} %get-tuple-element.328, bf16[1,1024,128]{1,2,0:T(8,128)(2,1)} %copy.56, f32[128]{0:T(128)} %get-tuple-element.377, f32[1024]{0:T(1024)S(1)} %add_rsqrt_fusion.4, ...), kind=kOutput, calls=%fused_computation.11.clone.1 | convolution fusion | flops 542507008 | bytes 2897409 | tf_op jit(solution)/shard_map/while/body/eval_jaxpr/dot_general | solution.py:245
  100.1 5.2 %convolution_add_fusion.5 = f32[1024,128]{1,0:T(8,128)} fusion(f32[1024,128]{1,0:T(8,128)} %fusion.131, bf16[4096,128]{1,0:T(8,128)(2,1)} %get-tuple-element.373, s32[1024]{0:T(1024)S(1)} %bitcast.98, bf16[384,128]{1,0:T(8,128)(2,1)S(1)} %get-tuple-element.371), kind=kOutput, calls=%fused_computation.13.clone.1 | convolution fusion | flops 1111752704 | bytes 2134016 | tf_op jit(solution)/shard_map/while/body/eval_jaxpr/dot_general | solution.py:226
  105.3 3.6 %multiply_convert_fusion.6 = bf16[1024,128]{1,0:T(8,128)(2,1)} fusion(f32[1024,128]{1,0:T(8,128)} %convolution_add_fusion.5, bf16[2048,128]{1,0:T(8,128)(2,1)} %get-tuple-element.374, s32[1024]{0:T(1024)S(1)} %bitcast.96, bf16[384,128]{1,0:T(8,128)(2,1)S(1)} %get-tuple-element.371), kind=kOutput, calls=%fused_computation.19.clone.1 | convolution fusion | flops 573440000 | bytes 1347584 | tf_op jit(solution)/shard_map/while/body/eval_jaxpr/dot_general | solution.py:231
  115.7 4.0 %fusion.133 = f32[2048,128]{1,0:T(8,128)} fusion(s32[1024]{0:T(1024)S(1)} %bitcast.97, f32[2048,128]{1,0:T(8,128)} %get-tuple-element.348, pred[]{:T(512)S(6)} %compare.14, f32[1024,128]{0,1:T(8,128)} %get-tuple-element.328, bf16[1,1024,128]{1,2,0:T(8,128)(2,1)} %copy.56, f32[128]{0:T(128)} %get-tuple-element.377, f32[1024]{0:T(1024)S(1)} %add_rsqrt_fusion.4, ...), kind=kOutput, calls=%fused_computation.11.clone.1 | convolution fusion | flops 542507008 | bytes 2897409 | tf_op jit(solution)/shard_map/while/body/eval_jaxpr/dot_general | solution.py:245
  122.5 5.2 %convolution_add_fusion.5 = f32[1024,128]{1,0:T(8,128)} fusion(f32[1024,128]{1,0:T(8,128)} %fusion.131, bf16[4096,128]{1,0:T(8,128)(2,1)} %get-tuple-element.373, s32[1024]{0:T(1024)S(1)} %bitcast.98, bf16[384,128]{1,0:T(8,128)(2,1)S(1)} %get-tuple-element.371), kind=kOutput, calls=%fused_computation.13.clone.1 | convolution fusion | flops 1111752704 | bytes 2134016 | tf_op jit(solution)/shard_map/while/body/eval_jaxpr/dot_general | solution.py:226
  127.7 3.6 %multiply_convert_fusion.6 = bf16[1024,128]{1,0:T(8,128)(2,1)} fusion(f32[1024,128]{1,0:T(8,128)} %convolution_add_fusion.5, bf16[2048,128]{1,0:T(8,128)(2,1)} %get-tuple-element.374, s32[1024]{0:T(1024)S(1)} %bitcast.96, bf16[384,128]{1,0:T(8,128)(2,1)S(1)} %get-tuple-element.371), kind=kOutput, calls=%fused_computation.19.clone.1 | convolution fusion | flops 573440000 | bytes 1347584 | tf_op jit(solution)/shard_map/while/body/eval_jaxpr/dot_general | solution.py:231
  138.1 4.0 %fusion.133 = f32[2048,128]{1,0:T(8,128)} fusion(s32[1024]{0:T(1024)S(1)} %bitcast.97, f32[2048,128]{1,0:T(8,128)} %get-tuple-element.348, pred[]{:T(512)S(6)} %compare.14, f32[1024,128]{0,1:T(8,128)} %get-tuple-element.328, bf16[1,1024,128]{1,2,0:T(8,128)(2,1)} %copy.56, f32[128]{0:T(128)} %get-tuple-element.377, f32[1024]{0:T(1024)S(1)} %add_rsqrt_fusion.4, ...), kind=kOutput, calls=%fused_computation.11.clone.1 | convolution fusion | flops 542507008 | bytes 2897409 | tf_op jit(solution)/shard_map/while/body/eval_jaxpr/dot_general | solution.py:245
  144.9 5.2 %convolution_add_fusion.5 = f32[1024,128]{1,0:T(8,128)} fusion(f32[1024,128]{1,0:T(8,128)} %fusion.131, bf16[4096,128]{1,0:T(8,128)(2,1)} %get-tuple-element.373, s32[1024]{0:T(1024)S(1)} %bitcast.98, bf16[384,128]{1,0:T(8,128)(2,1)S(1)} %get-tuple-element.371), kind=kOutput, calls=%fused_computation.13.clone.1 | convolution fusion | flops 1111752704 | bytes 2134016 | tf_op jit(solution)/shard_map/while/body/eval_jaxpr/dot_general | solution.py:226
  150.1 3.6 %multiply_convert_fusion.6 = bf16[1024,128]{1,0:T(8,128)(2,1)} fusion(f32[1024,128]{1,0:T(8,128)} %convolution_add_fusion.5, bf16[2048,128]{1,0:T(8,128)(2,1)} %get-tuple-element.374, s32[1024]{0:T(1024)S(1)} %bitcast.96, bf16[384,128]{1,0:T(8,128)(2,1)S(1)} %get-tuple-element.371), kind=kOutput, calls=%fused_computation.19.clone.1 | convolution fusion | flops 573440000 | bytes 1347584 | tf_op jit(solution)/shard_map/while/body/eval_jaxpr/dot_general | solution.py:231
  160.5 4.0 %fusion.133 = f32[2048,128]{1,0:T(8,128)} fusion(s32[1024]{0:T(1024)S(1)} %bitcast.97, f32[2048,128]{1,0:T(8,128)} %get-tuple-element.348, pred[]{:T(512)S(6)} %compare.14, f32[1024,128]{0,1:T(8,128)} %get-tuple-element.328, bf16[1,1024,128]{1,2,0:T(8,128)(2,1)} %copy.56, f32[128]{0:T(128)} %get-tuple-element.377, f32[1024]{0:T(1024)S(1)} %add_rsqrt_fusion.4, ...), kind=kOutput, calls=%fused_computation.11.clone.1 | convolution fusion | flops 542507008 | bytes 2897409 | tf_op jit(solution)/shard_map/while/body/eval_jaxpr/dot_general | solution.py:245
  167.3 5.2 %convolution_add_fusion.5 = f32[1024,128]{1,0:T(8,128)} fusion(f32[1024,128]{1,0:T(8,128)} %fusion.131, bf16[4096,128]{1,0:T(8,128)(2,1)} %get-tuple-element.373, s32[1024]{0:T(1024)S(1)} %bitcast.98, bf16[384,128]{1,0:T(8,128)(2,1)S(1)} %get-tuple-element.371), kind=kOutput, calls=%fused_computation.13.clone.1 | convolution fusion | flops 1111752704 | bytes 2134016 | tf_op jit(solution)/shard_map/while/body/eval_jaxpr/dot_general | solution.py:226
  172.5 3.6 %multiply_convert_fusion.6 = bf16[1024,128]{1,0:T(8,128)(2,1)} fusion(f32[1024,128]{1,0:T(8,128)} %convolution_add_fusion.5, bf16[2048,128]{1,0:T(8,128)(2,1)} %get-tuple-element.374, s32[1024]{0:T(1024)S(1)} %bitcast.96, bf16[384,128]{1,0:T(8,128)(2,1)S(1)} %get-tuple-element.371), kind=kOutput, calls=%fused_computation.19.clone.1 | convolution fusion | flops 573440000 | bytes 1347584 | tf_op jit(solution)/shard_map/while/body/eval_jaxpr/dot_general | solution.py:231
  182.9 4.0 %fusion.133 = f32[2048,128]{1,0:T(8,128)} fusion(s32[1024]{0:T(1024)S(1)} %bitcast.97, f32[2048,128]{1,0:T(8,128)} %get-tuple-element.348, pred[]{:T(512)S(6)} %compare.14, f32[1024,128]{0,1:T(8,128)} %get-tuple-element.328, bf16[1,1024,128]{1,2,0:T(8,128)(2,1)} %copy.56, f32[128]{0:T(128)} %get-tuple-element.377, f32[1024]{0:T(1024)S(1)} %add_rsqrt_fusion.4, ...), kind=kOutput, calls=%fused_computation.11.clone.1 | convolution fusion | flops 542507008 | bytes 2897409 | tf_op jit(solution)/shard_map/while/body/eval_jaxpr/dot_general | solution.py:245
  186.9 7.5 %all-reduce.4 = (bf16[2048,128]{1,0:T(8,128)(2,1)}, f32[8]{0:T(128)S(1)}) all-reduce(f32[2048,128]{1,0:T(8,128)} %get-tuple-element.99, f32[8]{0:T(128)} %copy-done.14), channel_id=1, replica_groups=mesh['dom'=64,'head'=2] {'head'}, use_global_device_ids=true, to_apply=%region_4.5 | all-reduce | flops 262152 | bytes 1572928 | tf_op jit(solution)/shard_map/psum | solution.py:254
  209.6 30.3 %shard_map.199 = f32[72,128]{1,0:T(8,128)} custom-call(f32[72,128]{1,0:T(8,128)} %fusion.67.x_ref), custom_call_target="tpu_custom_call" | custom-call | tf_op jit(solution)/shard_map/pallas_call | solution.py:52
  (163 shorter events, 123.1 us)
Async XLA Ops:
  0.0 24.9 %copy-start = (bf16[12288,128]{1,0:T(8,128)(2,1)S(1)}, bf16[12288,128]{1,0:T(8,128)(2,1)}, u32[]{:S(2)}) copy-start(bf16[12288,128]{1,0:T(8,128)(2,1)} %param.26) | copy-start | bytes 9437188
  0.0 12.0 %copy-start.4 = (bf16[2048,128]{1,0:T(8,128)(2,1)S(1)}, bf16[2048,128]{1,0:T(8,128)(2,1)}, u32[]{:S(2)}) copy-start(bf16[2048,128]{1,0:T(8,128)(2,1)} %param.25) | copy-start | bytes 1572868
  0.9 21.6 %copy-start.12 = (bf16[256,128]{1,0:T(8,128)(2,1)S(1)}, bf16[256,128]{1,0:T(8,128)(2,1)}, u32[]{:S(2)}) copy-start(bf16[256,128]{1,0:T(8,128)(2,1)} %param.35) | copy-start | bytes 196612
  3.6 43.4 %collective-permute-start = (bf16[512,128]{1,0:T(8,128)(2,1)}, bf16[512,128]{1,0:T(8,128)(2,1)}, u32[]{:S(2)}, u32[]{:S(2)}) collective-permute-start(bf16[512,128]{1,0:T(8,128)(2,1)} %fusion.50), channel_id=1, source_target_pairs={{0,2},{2,4},{4,6},{6,8},{8,10},{10,12},{12,14},{14,16},{16,18},{18... | collective-permute-start | bytes 393224 | tf_op jit(solution)/shard_map/ppermute | solution.py:18
  9.9 38.7 %collective-permute-start.1 = (bf16[512,128]{1,0:T(8,128)(2,1)}, bf16[512,128]{1,0:T(8,128)(2,1)}, u32[]{:S(2)}, u32[]{:S(2)}) collective-permute-start(bf16[512,128]{1,0:T(8,128)(2,1)} %fusion.49), channel_id=1, source_target_pairs={{2,0},{4,2},{6,4},{8,6},{10,8},{12,10},{14,12},{16,14},{18,16},{20... | collective-permute-start | bytes 393224 | tf_op jit(solution)/shard_map/ppermute | solution.py:18
  13.5 36.6 %collective-permute-start.2 = (bf16[512,128]{1,0:T(8,128)(2,1)}, bf16[512,128]{1,0:T(8,128)(2,1)S(1)}, u32[]{:S(2)}, u32[]{:S(2)}) collective-permute-start(bf16[512,128]{1,0:T(8,128)(2,1)} %fusion.48), channel_id=1, source_target_pairs={{0,4},{2,6},{4,8},{6,10},{8,12},{10,14},{12,16},{14,18},{16,20},{1... | collective-permute-start | bytes 393224 | tf_op jit(solution)/shard_map/ppermute | solution.py:18
  18.2 13.4 %copy-start.17 = (u32[128]{0:T(128)S(1)}, u32[128]{0:T(128)}, u32[]{:S(2)}) copy-start(u32[128]{0:T(128)} %constant.89) | copy-start | bytes 1540
  18.2 14.7 %copy-start.16 = (f32[4]{0:T(128)S(1)}, f32[4]{0:T(128)}, u32[]{:S(2)}) copy-start(f32[4]{0:T(128)} %param.42) | copy-start | bytes 52
  19.7 18.6 %copy-start.9 = (bf16[128,256]{1,0:T(8,128)(2,1)S(1)}, bf16[128,256]{1,0:T(8,128)(2,1)}, u32[]{:S(2)}) copy-start(bf16[128,256]{1,0:T(8,128)(2,1)} %param.41) | copy-start | bytes 196612
  19.7 31.1 %collective-permute-start.3 = (bf16[512,128]{1,0:T(8,128)(2,1)}, bf16[512,128]{1,0:T(8,128)(2,1)}, u32[]{:S(2)}, u32[]{:S(2)}) collective-permute-start(bf16[512,128]{1,0:T(8,128)(2,1)} %fusion.47), channel_id=1, source_target_pairs={{4,0},{6,2},{8,4},{10,6},{12,8},{14,10},{16,12},{18,14},{20,16},{2... | collective-permute-start | bytes 393224 | tf_op jit(solution)/shard_map/ppermute | solution.py:18
  22.5 30.4 %copy-start.6 = (bf16[384,128]{1,0:T(8,128)(2,1)S(1)}, bf16[384,128]{1,0:T(8,128)(2,1)}, u32[]{:S(2)}) copy-start(bf16[384,128]{1,0:T(8,128)(2,1)} %param.31) | copy-start | bytes 294916
  24.9 5.2 %dynamic-slice-start.1 = ((s32[12288]{0:T(1024)}, s32[]{:T(128)}), s32[6144]{0:T(1024)S(1)}, s32[]{:S(2)}) async-start(s32[12288]{0:T(1024)} %param.28, s32[]{:T(128)} %select_n.9), calls=%async_computation.1 | async-start | bytes 49664 | tf_op jit(solution)/shard_map/dynamic_slice | solution.py:207
  24.9 5.2 %dynamic-slice-start = ((s32[12288]{0:T(1024)}, s32[]{:T(128)}), s32[6144]{0:T(1024)S(1)}, s32[]{:S(2)}) async-start(s32[12288]{0:T(1024)} %param.27, s32[]{:T(128)} %select_n.9), calls=%async_computation | async-start | bytes 49664 | tf_op jit(solution)/shard_map/dynamic_slice | solution.py:206
  33.1 19.8 %copy-start.14 = (f32[8]{0:T(128)}, f32[8]{0:T(128)S(1)}, u32[]{:S(2)}) copy-start(f32[8]{0:T(128)S(1)} %dynamic-update-slice.2) | copy-start | bytes 100
  194.5 2.9 %copy-start.10 = (bf16[128,128]{1,0:T(8,128)(2,1)S(1)}, bf16[128,128]{1,0:T(8,128)(2,1)}, u32[]{:S(2)}) copy-start(bf16[128,128]{1,0:T(8,128)(2,1)} %param.37) | copy-start | bytes 98308
  194.5 4.5 %copy-start.13 = (f32[128]{0:T(128)S(1)}, f32[128]{0:T(128)}, u32[]{:S(2)}) copy-start(f32[128]{0:T(128)} %param.38) | copy-start | bytes 1540
  197.4 3.2 %copy-start.11 = (bf16[128,128]{0,1:T(8,128)(2,1)S(1)}, bf16[128,128]{0,1:T(8,128)(2,1)}, u32[]{:S(2)}) copy-start(bf16[128,128]{0,1:T(8,128)(2,1)} %all-gather) | copy-start | bytes 98308
  197.4 3.2 %copy-start.15 = (f32[128]{0:T(128)S(1)}, f32[128]{0:T(128)}, u32[]{:S(2)}) copy-start(f32[128]{0:T(128)} %param.39) | copy-start | bytes 1540
  197.4 3.7 %copy-start.5 = (bf16[128,512]{1,0:T(8,128)(2,1)S(1)}, bf16[128,512]{1,0:T(8,128)(2,1)}, u32[]{:S(2)}) copy-start(bf16[128,512]{1,0:T(8,128)(2,1)} %all-gather.1) | copy-start | bytes 393220
  200.3 0.8 copy-start.2
  201.9 1.9 copy-start.1
  205.6 3.3 %copy-start.8 = (f32[8192]{0:T(1024)S(1)}, f32[8192]{0:T(1024)}, u32[]{:S(2)}) copy-start(f32[8192]{0:T(1024)} %reshape.126) | copy-start | bytes 98308
  248.0 3.2 %copy-start.3 = (bf16[2048,128]{0,1:T(8,128)(2,1)S(1)}, bf16[2048,128]{0,1:T(8,128)(2,1)}, u32[]{:S(2)}) copy-start(bf16[2048,128]{0,1:T(8,128)(2,1)} %copy-done.2) | copy-start | bytes 1572868
  248.0 3.2 %copy-start.7 = (bf16[128,128]{1,0:T(8,128)(2,1)S(1)}, bf16[128,128]{1,0:T(8,128)(2,1)}, u32[]{:S(2)}) copy-start(bf16[128,128]{1,0:T(8,128)(2,1)} %all-gather.5) | copy-start | bytes 98308
